TPU v7x, 32 devices: a whole 2x2x4 slice. The times are simulated.
32 devices in a mesh: pipe: 4 (over x, core), row: 4 (over z), col: 2 (over y).
Axes of the slice: x: 2, y: 2, z: 4, core: 2. Of those that a mesh axis runs over, the one named last changes fastest.
Arguments:
- handoff: bfloat16 [4, 256, 12288], P('pipe', 'col', 'row'), may hold values from -1200 to 1200
- norm_gain: float32 [4, 12288], P('pipe', 'row'), may hold values from 0.1 to 1.9
- norm_shift: float32 [4, 12288], P('pipe', 'row'), may hold values from -3 to 3
- up_weight: bfloat16 [4, 12288, 24576], P('pipe', 'row', 'col'), may hold values from -0.0546875 to 0.0546875
- up_bias: float32 [4, 24576], P('pipe', 'col'), may hold values from -3 to 3
Outputs:
- hidden: bfloat16 [4, 256, 24576], P('pipe', 'row', 'col')
All inputs are finite; a program needn't handle non-finite values.
Results may differ from a plain program's by a relative error of at most 0.018.
Values may be sent and summed in bfloat16 or wider, within the bound.
A program may use at most 128 MiB of HBM per device.

v0:
```python
import jax
import jax.numpy as jnp
from jax import lax
from jax.sharding import PartitionSpec as P

epsilon = 1e-05


def passed_along(value, axis, steps):
    count = lax.axis_size(axis)
    pairs = [(source, (source + steps) % count) for source in range(count)]
    return lax.ppermute(value, axis, pairs)


def normalize(values, row_total, squares, feature_gain, feature_shift, feature_count):
    center = (row_total / feature_count)[:, None]
    spread_sq = (squares / feature_count)[:, None] - center * center
    inverse = lax.rsqrt(spread_sq + epsilon)
    return ((values - center) * inverse * feature_gain + feature_shift).astype(jnp.bfloat16)


def local(handoff, norm_gain, norm_shift, up_weight, up_bias):
    arrived = passed_along(handoff[0], "pipe", 1)
    feature_gain = norm_gain[0]
    feature_shift = norm_shift[0]
    weight_block = up_weight[0]
    bias_block = up_bias[0]
    feature_count = arrived.shape[1] * lax.axis_size("row")
    values = arrived.astype(jnp.float32)
    row_total, squares = lax.psum(
        (jnp.sum(values, axis=1), jnp.sum(values * values, axis=1)), "row"
    )
    own_normed = normalize(values, row_total, squares, feature_gain, feature_shift, feature_count)
    normed = lax.all_gather(own_normed, "col", axis=0, tiled=True)
    summed = lax.psum_scatter(
        jnp.dot(normed, weight_block, preferred_element_type=jnp.float32).astype(jnp.bfloat16),
        "row",
        scatter_dimension=0,
        tiled=True,
    ).astype(jnp.float32)
    preact = summed + bias_block
    return jax.nn.gelu(preact, approximate=True).astype(jnp.bfloat16)[None]


def solution(mesh):
    in_specs = (
        P("pipe", "col", "row"),
        P("pipe", "row"),
        P("pipe", "row"),
        P("pipe", "row", "col"),
        P("pipe", "col"),
    )
    out_specs = P("pipe", "row", "col")
    return jax.shard_map(local, mesh=mesh, in_specs=in_specs, out_specs=out_specs, check_vma=False)
```

profile of v0, /device:TPU:0, one launch (start us, length us, event | category | flops | bytes accessed | tf_op | source)
XLA Modules:
  0.0 212.2 jit_solution(13344893527006407649)
XLA Ops:
  6.5 0.0 all-gather.2.cloned.1.call-start
  6.5 0.5 collective-permute-start
  7.0 11.8 %collective-permute-done = bf16[128,3072]{1,0:T(8,128)(2,1)S(1)} collective-permute-done((bf16[128,3072]{1,0:T(8,128)(2,1)}, bf16[128,3072]{1,0:T(8,128)(2,1)S(1)}, u32[]{:S(2)}, u32[]{:S(2)}) %collective-permute-start) | collective-permute-done | bytes 786464 | tf_op jit(solution)/shard_map/ppermute | solution.py:12
  18.8 0.3 convert_reduce_fusion
  19.1 12.8 %all-reduce = (f32[128]{0:T(128)S(1)}, f32[128]{0:T(128)S(1)}) all-reduce(f32[128]{0:T(128)S(1)} %get-tuple-element.6, f32[128]{0:T(128)S(1)} %get-tuple-element.5), channel_id=1, replica_groups=mesh['pipe'=4,'row'=4,'col'=2] {'row'}, use_global_device_ids=true, to_apply=%region_3.0 | all-reduce | flops 256 | bytes 2048 | tf_op jit(solution)/shard_map/psum | solution.py:30
  31.9 2.0 fusion.16
  33.9 0.0 all-gather.2.cloned.1.call-update
  33.9 0.0 reduce-scatter.2.cloned.1.call-start
  34.0 25.5 %all-gather.2.cloned.1.call-done = bf16[256,3072]{1,0:T(8,128)(2,1)} async-done(((bf16[128,3072]{1,0:T(8,128)(2,1)}), bf16[256,3072]{1,0:T(8,128)(2,1)}) %all-gather.2.cloned.1.call-update) | async-done | bytes 1572880 | tf_op jit(solution)/shard_map/all_gather | solution.py:34
  59.5 31.2 %fusion.2 = bf16[256,12288]{1,0:T(8,128)(2,1)} fusion(bf16[256,3072]{1,0:T(8,128)(2,1)} %all-gather.2.cloned.1.call-done, bf16[1,3072,12288]{2,1,0:T(8,128)(2,1)} %param.8), kind=kOutput, calls=%fused_computation.2 | convolution fusion | flops 19330498560 | bytes 83361792 | tf_op jit(solution)/shard_map/dot_general | solution.py:36
  90.6 0.0 copy-start
  90.6 0.0 reduce-scatter.2.cloned.1.call-update
  90.7 110.9 %reduce-scatter.2.cloned.1.call-done = bf16[64,12288]{1,0:T(8,128)(2,1)} async-done(((bf16[256,12288]{1,0:T(8,128)(2,1)}), bf16[64,12288]{1,0:T(8,128)(2,1)}) %reduce-scatter.2.cloned.1.call-update) | async-done | bytes 1572880 | tf_op jit(solution)/shard_map/reduce_scatter | solution.py:35
  201.6 0.0 copy-done
  201.6 3.7 %fusion.18 = bf16[1,64,12288]{2,1,0:T(8,128)(2,1)} fusion(bf16[64,12288]{1,0:T(8,128)(2,1)} %reduce-scatter.2.cloned.1.call-done, f32[12288]{0:T(1024)S(1)} %bitcast.12), kind=kLoop, calls=%fused_computation.20 | loop fusion | flops 8650752 | bytes 3194880 | tf_op jit(solution)/shard_map/broadcast_in_dim | solution.py:42
  (1 shorter events, 0.0 us)
Async XLA Ops:
  6.5 52.9 %all-gather.2.cloned.1.call-start = ((), (), s32[]{:S(2)}) async-start(), calls=%async_computation.1 | async-start | bytes 2359296 | tf_op jit(solution)/shard_map/all_gather | solution.py:34
  6.5 12.3 %collective-permute-start = (bf16[128,3072]{1,0:T(8,128)(2,1)}, bf16[128,3072]{1,0:T(8,128)(2,1)S(1)}, u32[]{:S(2)}, u32[]{:S(2)}) collective-permute-start(bf16[128,3072]{1,0:T(8,128)(2,1)} %bitcast.15), channel_id=1, source_target_pairs={{0,8},{8,16},{16,24},{24,0},{1,9},{9,17},{17,25},{25,1},{2,10},{10... | collective-permute-start | bytes 2359304 | tf_op jit(solution)/shard_map/ppermute | solution.py:12
  33.9 167.7 %reduce-scatter.2.cloned.1.call-start = ((), (), s32[]{:S(2)}) async-start(), calls=%async_computation.2 | async-start | bytes 7864320 | tf_op jit(solution)/shard_map/reduce_scatter | solution.py:35
  90.6 111.0 %copy-start = (f32[1,12288]{1,0:T(1,128)S(1)}, f32[1,12288]{1,0:T(1,128)}, u32[]{:S(2)}) copy-start(f32[1,12288]{1,0:T(1,128)} %param.9) | copy-start | bytes 147460
Sparse Core Ops, SparseCore 0:
  34.0 25.3 all-gather.1
  90.8 110.7 reduce-scatter.1
where the time goes:
time: 212 us
  waiting for transfers between devices  148 us (70%)
  matrix products  31.2 us (15%)
  between operations  13.4 us (6%)
  blocking collectives  12.8 us (6%)
  other arithmetic  6.01 us (3%)
    reduce_scatter x1, waiting for transfers between devices, local(): lax.psum_scatter(jnp.dot(normed, weight_block, preferred_element_type=jnp...  111 us
    dot_general x1, matrix products, local(): jnp.dot(normed, weight_block, preferred_element_type=jnp.float32)  31.2 us
    all_gather x1, waiting for transfers between devices, local(): normed = lax.all_gather(own_normed, 'col', axis=0, tiled=True)  25.5 us
    psum x1, blocking collectives, local(): lax.psum((jnp.sum(values, axis=1), jnp.sum(values * values, axis=1)), 'row')  12.8 us
    ppermute x1, waiting for transfers between devices, passed_along(): return lax.ppermute(value, axis, pairs)  11.8 us
  transfers between devices with their start and end apart: 3, of which 3 were waited for; matrix products, arithmetic and copies ran while one was open for 0% of the time, Pallas kernels for 0%

commit v1 on v0

--- a/solution.py
+++ b/solution.py
@@ -4,6 +4,24 @@
 from jax.sharding import PartitionSpec as P
 
 epsilon = 1e-05
+
+
+def laid_out(blocks, dim):
+    blocks = jnp.moveaxis(blocks, 0, dim)
+    dims = blocks.shape
+    return blocks.reshape(*dims[:dim], dims[dim] * dims[dim + 1], *dims[dim + 2 :])
+
+
+def collected_by_bits(value, axis):
+    peers = lax.axis_size(axis)
+    blocks = value[None]
+    for level in range(peers.bit_length() - 1):
+        bit = 1 << level
+        other = lax.ppermute(blocks, axis, [(i, i ^ bit) for i in range(peers)])
+        both = jnp.stack([blocks, other])
+        upper = lax.axis_index(axis) >> level & 1
+        blocks = jnp.where(upper == 0, both, both[::-1]).reshape(-1, *value.shape)
+    return blocks
 
 
 def passed_along(value, axis, steps):
@@ -31,7 +49,7 @@
         (jnp.sum(values, axis=1), jnp.sum(values * values, axis=1)), "row"
     )
     own_normed = normalize(values, row_total, squares, feature_gain, feature_shift, feature_count)
-    normed = lax.all_gather(own_normed, "col", axis=0, tiled=True)
+    normed = laid_out(collected_by_bits(own_normed, "col"), 0)
     summed = lax.psum_scatter(
         jnp.dot(normed, weight_block, preferred_element_type=jnp.float32).astype(jnp.bfloat16),
         "row",

time: 212 us -> 202 us (0.953)
  waiting for transfers between devices: 148 us -> 135 us
    all_gather x1 -> x0, waiting for transfers between devices: 25.5 us -> none  [local(): normed = lax.all_gather(own_normed, 'col', axis=0, tiled=True)]
    ppermute x0 -> x1, waiting for transfers between devices: none -> 15.1 us  [collected_by_bits(): other = lax.ppermute(blocks, axis, [(i, i ^ bit) for i in range(peers)])]
    reduce_scatter x1, waiting for transfers between devices: 111 us -> 108 us  [local(): lax.psum_scatter(jnp.dot(normed, weight_block, preferred_element_type=jnp...]
where the time goes in v1:
time: 202 us; the launch traced here: 201 us
  waiting for transfers between devices  135 us (67%)
  matrix products  32.1 us (16%)
  between operations  13.4 us (7%)
  blocking collectives  12.8 us (6%)
  other arithmetic  5.68 us (3%)
  starting transfers between devices  2.08 us (1%)
    reduce_scatter x1, waiting for transfers between devices, local(): lax.psum_scatter(jnp.dot(normed, weight_block, preferred_element_type=jnp...  108 us
    dot_general x1, matrix products, local(): jnp.dot(normed, weight_block, preferred_element_type=jnp.float32)  32.1 us
    ppermute x1, waiting for transfers between devices, collected_by_bits(): other = lax.ppermute(blocks, axis, [(i, i ^ bit) for i in range(peers)])  15.1 us
    psum x1, blocking collectives, local(): lax.psum((jnp.sum(values, axis=1), jnp.sum(values * values, axis=1)), 'row')  12.8 us
    ppermute x1, waiting for transfers between devices, passed_along(): return lax.ppermute(value, axis, pairs)  11.8 us
  transfers between devices with their start and end apart: 3, of which 3 were waited for; matrix products, arithmetic and copies ran while one was open for 0% of the time, Pallas kernels for 0%

profile of v1, /device:TPU:0, one launch (start us, length us, event | category | flops | bytes accessed | tf_op | source)
XLA Modules:
  0.0 201.2 jit_solution(7908120483561139065)
XLA Ops:
  6.5 0.0 reduce-scatter.2.cloned.1.call-start
  6.5 0.5 collective-permute-start
  7.0 11.8 %collective-permute-done = bf16[128,3072]{1,0:T(8,128)(2,1)S(1)} collective-permute-done((bf16[128,3072]{1,0:T(8,128)(2,1)}, bf16[128,3072]{1,0:T(8,128)(2,1)S(1)}, u32[]{:S(2)}, u32[]{:S(2)}) %collective-permute-start) | collective-permute-done | bytes 786464 | tf_op jit(solution)/shard_map/ppermute | solution.py:30
  18.8 0.3 convert_reduce_fusion
  19.1 12.8 %all-reduce = (f32[128]{0:T(128)S(1)}, f32[128]{0:T(128)S(1)}) all-reduce(f32[128]{0:T(128)S(1)} %get-tuple-element.6, f32[128]{0:T(128)S(1)} %get-tuple-element.5), channel_id=1, replica_groups=mesh['pipe'=4,'row'=4,'col'=2] {'row'}, use_global_device_ids=true, to_apply=%region_3.0 | all-reduce | flops 256 | bytes 2048 | tf_op jit(solution)/shard_map/psum | solution.py:48
  31.9 1.2 fusion.20
  33.1 1.6 collective-permute-start.1
  34.7 15.1 %collective-permute-done.1 = bf16[1,128,3072]{2,1,0:T(8,128)(2,1)S(1)} collective-permute-done((bf16[1,128,3072]{2,1,0:T(8,128)(2,1)S(1)}, bf16[1,128,3072]{2,1,0:T(8,128)(2,1)S(1)}, u32[]{:S(2)}, u32[]{:S(2)}) %collective-permute-start.1) | collective-permute-done | bytes 786464 | tf_op jit(solution)/shard_map/ppermute | solution.py:20
  49.8 0.1 pad_maximum_fusion
  50.0 0.3 reverse_select_fusion
  50.3 32.1 %fusion.2 = bf16[256,12288]{1,0:T(8,128)(2,1)} fusion(bf16[256,3072]{1,0:T(8,128)(2,1)S(1)} %bitcast.18, bf16[1,3072,12288]{2,1,0:T(8,128)(2,1)} %param.8), kind=kOutput, calls=%fused_computation.2 | convolution fusion | flops 19330498560 | bytes 83361792 | tf_op jit(solution)/shard_map/dot_general | solution.py:54
  82.4 0.0 copy-start
  82.4 0.0 reduce-scatter.2.cloned.1.call-update
  82.4 108.2 %reduce-scatter.2.cloned.1.call-done = bf16[64,12288]{1,0:T(8,128)(2,1)} async-done(((bf16[256,12288]{1,0:T(8,128)(2,1)}), bf16[64,12288]{1,0:T(8,128)(2,1)}) %reduce-scatter.2.cloned.1.call-update) | async-done | bytes 1572880 | tf_op jit(solution)/shard_map/reduce_scatter | solution.py:53
  190.6 0.0 copy-done
  190.6 3.7 %fusion.18 = bf16[1,64,12288]{2,1,0:T(8,128)(2,1)} fusion(bf16[64,12288]{1,0:T(8,128)(2,1)} %reduce-scatter.2.cloned.1.call-done, f32[12288]{0:T(1024)S(1)} %bitcast.20), kind=kLoop, calls=%fused_computation.21 | loop fusion | flops 8650752 | bytes 3194880 | tf_op jit(solution)/shard_map/broadcast_in_dim | solution.py:60
  (1 shorter events, 0.0 us)
Async XLA Ops:
  6.5 184.1 %reduce-scatter.2.cloned.1.call-start = ((), (), s32[]{:S(2)}) async-start(), calls=%async_computation.1 | async-start | bytes 7864320 | tf_op jit(solution)/shard_map/reduce_scatter | solution.py:53
  6.5 12.3 %collective-permute-start = (bf16[128,3072]{1,0:T(8,128)(2,1)}, bf16[128,3072]{1,0:T(8,128)(2,1)S(1)}, u32[]{:S(2)}, u32[]{:S(2)}) collective-permute-start(bf16[128,3072]{1,0:T(8,128)(2,1)} %bitcast.23), channel_id=1, source_target_pairs={{0,8},{8,16},{16,24},{24,0},{1,9},{9,17},{17,25},{25,1},{2,10},{10... | collective-permute-start | bytes 2359304 | tf_op jit(solution)/shard_map/ppermute | solution.py:30
  33.1 16.7 %collective-permute-start.1 = (bf16[1,128,3072]{2,1,0:T(8,128)(2,1)S(1)}, bf16[1,128,3072]{2,1,0:T(8,128)(2,1)S(1)}, u32[]{:S(2)}, u32[]{:S(2)}) collective-permute-start(bf16[1,128,3072]{2,1,0:T(8,128)(2,1)S(1)} %get-tuple-element.10), channel_id=1, source_target_pairs={{0,1},{1,0},{2,3},{3,2},{4,5},{5,4},{6,7},{7,6},{8,9},{9,8},{10,11... | collective-permute-start | bytes 2359304 | tf_op jit(solution)/shard_map/ppermute | solution.py:20
  82.4 108.2 %copy-start = (f32[1,12288]{1,0:T(1,128)S(1)}, f32[1,12288]{1,0:T(1,128)}, u32[]{:S(2)}) copy-start(f32[1,12288]{1,0:T(1,128)} %param.9) | copy-start | bytes 147460
Sparse Core Ops, SparseCore 0:
  82.5 108.0 reduce-scatter.1
